TPU v7x, 512 devices: a whole 4x8x8 slice. The times are simulated.
512 devices in a mesh: row: 8 (over z), col: 8 (over x, y_hi), pair: 8 (over y_lo, core).
Axes of the slice: x: 4, y: 8 (y_hi: 2, y_lo: 4; y = y_hi * 4 + y_lo), z: 8, core: 2. Of those that a mesh axis runs over, the one named last changes fastest.
Arguments:
- pair_slab: bfloat16 [3072, 16384], P('pair', 'row'), may hold values from -0.4375 to 0.4375
- pair_weights: float32 [3072], P('pair'), may hold values from 0.2 to 2
Outputs:
- polarizability: float32 [16384, 16384], P('row', ('col', 'pair'))
All inputs are finite; a program needn't handle non-finite values.
Results may differ from a plain program's by a relative error of at most 0.0085.
Values may be sent and summed in bfloat16 or wider, within the bound.
A program may use at most 64 MiB of HBM per device.

v0:
```python
import jax
import jax.numpy as jnp
from jax import lax
from jax.sharding import PartitionSpec as P


def from_root(block, axis, owner):
    block = jnp.where(lax.axis_index(axis) == owner, block, jnp.zeros_like(block))
    return lax.psum(block, axis)


def contract_pairs(left, right):
    return lax.dot_general(
        left, right, (((0,), (0,)), ((), ())), preferred_element_type=jnp.float32
    )


def on_device(pair_slab, pair_weights):
    col_index = lax.axis_index("col")
    column_block = from_root(pair_slab, "row", col_index)
    own_columns = lax.all_to_all(column_block, "pair", split_axis=1, concat_axis=0, tiled=True)
    rows_piece = lax.all_gather(pair_slab, "pair", axis=0, tiled=True)
    weight_piece = lax.all_gather(
        pair_weights.astype(jnp.bfloat16), "pair", axis=0, tiled=True
    ).astype(jnp.float32)
    weighted = (weight_piece[:, None] * rows_piece.astype(jnp.float32)).astype(jnp.bfloat16)
    return contract_pairs(weighted, own_columns)


def solution(mesh):
    placed = (P("pair", "row"), P("pair"))
    return jax.shard_map(
        on_device, mesh=mesh, in_specs=placed, out_specs=P("row", ("col", "pair")), check_vma=False
    )
```

profile of v0, /device:TPU:9, one launch (start us, length us, event | category | flops | bytes accessed | tf_op | source)
XLA Modules:
  0.0 204.4 jit_solution(2897368251389527808)
XLA Ops:
  7.4 0.0 all-reduce.2.cloned.1.call-start
  7.4 1.9 copy.5
  9.3 1.3 broadcast_select_fusion
  10.5 0.0 all-reduce.2.cloned.1.call-update
  10.6 0.0 all-gather.3.cloned.1.call-start
  10.6 0.5 all-gather.3.cloned.1.call-update
  11.2 0.0 copy-start
  11.2 85.3 %all-reduce.2.cloned.1.call-done = bf16[384,8,256]{0,2,1:T(8,128)(2,1)} async-done(((bf16[384,8,256]{0,2,1:T(8,128)(2,1)}), bf16[384,8,256]{0,2,1:T(8,128)(2,1)}) %all-reduce.2.cloned.1.call-update) | async-done | bytes 1572880 | tf_op jit(solution)/shard_map/psum | solution.py:9
  96.5 9.2 %all-to-all-start = ((bf16[384,8,256]{0,2,1:T(8,128)(2,1)}), bf16[384,8,256]{0,2,1:T(8,128)(2,1)S(1)}, u32[]{:S(2)}, u32[]{:S(2)}) async-start(bf16[384,8,256]{0,2,1:T(8,128)(2,1)} %all-reduce.2.cloned.1.call-done), calls=%async_computation | async-start | bytes 3145728 | tf_op jit(solution)/shard_map/all_to_all | solution.py:21
  105.7 0.0 copy-done
  105.7 65.9 %all-gather = bf16[8,1,384]{2,1,0:T(2,128)(2,1)S(1)} all-gather(bf16[1,1,384]{2,1,0:T(2,128)(2,1)S(1)} %reshape.4), channel_id=1, replica_groups=mesh['row'=8,'col'=8,'pair'=8] {'pair'}, dimensions={0}, use_global_device_ids=true | all-gather | bytes 6912 | tf_op jit(solution)/shard_map/all_gather | solution.py:23
  171.6 0.0 all-to-all-done
  171.7 0.8 copy.6
  172.4 13.9 %all-gather.3.cloned.1.call-done = bf16[3072,2048]{1,0:T(8,128)(2,1)} async-done(((bf16[384,2048]{1,0:T(8,128)(2,1)}), bf16[3072,2048]{1,0:T(8,128)(2,1)}) %all-gather.3.cloned.1.call-update) | async-done | bytes 12582928 | tf_op jit(solution)/shard_map/all_gather | solution.py:22
  186.3 10.6 %fusion = f32[2048,256]{1,0:T(8,128)} fusion(bf16[3072,256]{1,0:T(8,128)(2,1)S(1)} %bitcast.7, bf16[3072,2048]{1,0:T(8,128)(2,1)} %all-gather.3.cloned.1.call-done, f32[3072]{0:T(1024)S(1)} %bitcast.8), kind=kOutput, calls=%fused_computation.1 | convolution fusion | flops 3240099840 | bytes 16265216 | tf_op jit(solution)/shard_map/dot_general | solution.py:13
  (3 shorter events, 0.0 us)
Async XLA Ops:
  7.4 89.1 %all-reduce.2.cloned.1.call-start = ((), (), s32[]{:S(2)}) async-start(), calls=%async_computation.2 | async-start | bytes 3145728 | tf_op jit(solution)/shard_map/psum | solution.py:9
  10.6 175.7 %all-gather.3.cloned.1.call-start = ((), (), s32[]{:S(2)}) async-start(), calls=%async_computation.1 | async-start | bytes 14155776 | tf_op jit(solution)/shard_map/all_gather | solution.py:22
  11.2 94.5 %copy-start = (f32[384]{0:T(512)S(1)}, f32[384]{0:T(512)}, u32[]{:S(2)}) copy-start(f32[384]{0:T(512)} %param.3) | copy-start | bytes 4612
  96.5 75.2 %all-to-all-start = ((bf16[384,8,256]{0,2,1:T(8,128)(2,1)}), bf16[384,8,256]{0,2,1:T(8,128)(2,1)S(1)}, u32[]{:S(2)}, u32[]{:S(2)}) async-start(bf16[384,8,256]{0,2,1:T(8,128)(2,1)} %all-reduce.2.cloned.1.call-done), calls=%async_computation | async-start | bytes 3145728 | tf_op jit(solution)/shard_map/all_to_all | solution.py:21
Sparse Core Ops, SparseCore 0:
  10.7 85.7 all-reduce.1
Sparse Core Ops, SparseCore 1:
  13.1 173.1 all-gather.2
where the time goes:
time: 205 us; the launch traced here: 204 us
  waiting for transfers between devices  99.8 us (49%)
  blocking collectives  65.9 us (32%)
  between operations  14.9 us (7%)
  matrix products  10.6 us (5%)
  starting transfers between devices  9.26 us (5%)
  local copies, waits for them, and re-layouts  2.63 us (1%)
    psum x1, waiting for transfers between devices, from_root(): return lax.psum(block, axis)  85.3 us
    all_gather x1, blocking collectives, on_device(): lax.all_gather(pair_weights.astype(jnp.bfloat16), 'pair', axis=0, tiled=T...  65.9 us
    all_gather x1, waiting for transfers between devices, on_device(): rows_piece = lax.all_gather(pair_slab, 'pair', axis=0, tiled=True)  13.9 us
    dot_general x1, matrix products, contract_pairs(): lax.dot_general(left, right, (((0,), (0,)), ((), ())), preferred_element_...  10.6 us
    all_to_all x1, starting transfers between devices, on_device(): lax.all_to_all(column_block, 'pair', split_axis=1, concat_axis=0, tiled=T...  9.21 us
  transfers between devices with their start and end apart: 3, of which 2 were waited for; matrix products, arithmetic and copies ran while one was open for 0% of the time, Pallas kernels for 0%

commit v1 on v0

--- a/solution.py
+++ b/solution.py
@@ -20,8 +20,11 @@
     column_block = from_root(pair_slab, "row", col_index)
     own_columns = lax.all_to_all(column_block, "pair", split_axis=1, concat_axis=0, tiled=True)
     rows_piece = lax.all_gather(pair_slab, "pair", axis=0, tiled=True)
-    weight_piece = lax.all_gather(
-        pair_weights.astype(jnp.bfloat16), "pair", axis=0, tiled=True
+    weight_piece = jnp.concatenate(
+        lax.all_to_all(
+            jnp.stack([pair_weights.astype(jnp.bfloat16)] * lax.axis_size("pair")), "pair", 0, 0
+        ),
+        axis=0,
     ).astype(jnp.float32)
     weighted = (weight_piece[:, None] * rows_piece.astype(jnp.float32)).astype(jnp.bfloat16)
     return contract_pairs(weighted, own_columns)

time: 205 us -> 205 us (level)
  blocking collectives: 65.9 us -> 12.3 us
  waiting for transfers between devices: 99.8 us -> 152 us
    all_gather x1 -> x0, blocking collectives: 65.9 us -> none  [on_device(): lax.all_gather(pair_weights.astype(jnp.bfloat16), 'pair', axis=0, tiled=T...]
    all_to_all x1, waiting for transfers between devices: 0.01 us -> 59 us  [on_device(): lax.all_to_all(column_block, 'pair', split_axis=1, concat_axis=0, tiled=T...]
    psum x1, waiting for transfers between devices: 85.3 us -> 71.7 us  [from_root(): return lax.psum(block, axis)]
    all_to_all x0 -> x1, blocking collectives: none -> 12.3 us  [on_device(): lax.all_to_all(jnp.stack([pair_weights.astype(jnp.bfloat16)] * lax.axis_s...]
    all_gather x1, waiting for transfers between devices: 13.9 us -> 20.7 us  [on_device(): rows_piece = lax.all_gather(pair_slab, 'pair', axis=0, tiled=True)]
  transfers between devices with their start and end apart: 3 -> 3, of which waited for: 2 -> 3; matrix products, arithmetic and copies ran while one was open for 0% -> 1% of each run, Pallas kernels for 0% -> 0%
where the time goes in v1:
time: 205 us; the launch traced here: 204 us
  waiting for transfers between devices  152 us (74%)
  between operations  14.9 us (7%)
  blocking collectives  12.3 us (6%)
  matrix products  10.6 us (5%)
  starting transfers between devices  9.26 us (5%)
  local copies, waits for them, and re-layouts  3.41 us (2%)
    psum x1, waiting for transfers between devices, from_root(): return lax.psum(block, axis)  71.7 us
    all_to_all x1, waiting for transfers between devices, on_device(): lax.all_to_all(column_block, 'pair', split_axis=1, concat_axis=0, tiled=T...  59 us
    all_gather x1, waiting for transfers between devices, on_device(): rows_piece = lax.all_gather(pair_slab, 'pair', axis=0, tiled=True)  20.7 us
    all_to_all x1, blocking collectives, on_device(): lax.all_to_all(jnp.stack([pair_weights.astype(jnp.bfloat16)] * lax.axis_s...  12.3 us
    dot_general x1, matrix products, contract_pairs(): lax.dot_general(left, right, (((0,), (0,)), ((), ())), preferred_element_...  10.6 us
    all_to_all x1, starting transfers between devices, on_device(): lax.all_to_all(column_block, 'pair', split_axis=1, concat_axis=0, tiled=T...  9.21 us
  transfers between devices with their start and end apart: 3, of which 3 were waited for; matrix products, arithmetic and copies ran while one was open for 1% of the time, Pallas kernels for 0%

profile of v1, /device:TPU:9, one launch (start us, length us, event | category | flops | bytes accessed | tf_op | source)
XLA Modules:
  0.0 204.3 jit_solution(17775802150731279791)
XLA Ops:
  7.4 0.0 all-reduce.2.cloned.1.call-start
  7.4 1.9 copy.3
  9.3 1.3 broadcast_select_fusion
  10.5 0.0 copy-start
  10.6 0.0 all-reduce.2.cloned.1.call-update
  10.6 0.0 all-gather.2.cloned.1.call-start
  10.6 0.5 all-gather.2.cloned.1.call-update
  11.2 0.1 copy-done
  11.2 0.5 broadcast.4
  11.8 0.7 reduce
  12.5 0.1 reshape.20
  12.5 12.3 %all_to_all.25 = bf16[8,2,192]{2,1,0:T(2,128)(2,1)S(1)} all-to-all(bf16[8,2,192]{2,1,0:T(2,128)(2,1)S(1)} %reshape.20), channel_id=1, replica_groups=mesh['row'=8,'col'=8,'pair'=8] {'pair'}, dimensions={0} | all-to-all | bytes 12288 | tf_op jit(solution)/shard_map/all_to_all | solution.py:24
  24.8 71.7 %all-reduce.2.cloned.1.call-done = bf16[384,8,256]{0,2,1:T(8,128)(2,1)} async-done(((bf16[384,8,256]{0,2,1:T(8,128)(2,1)}), bf16[384,8,256]{0,2,1:T(8,128)(2,1)}) %all-reduce.2.cloned.1.call-update) | async-done | bytes 1572880 | tf_op jit(solution)/shard_map/psum | solution.py:9
  96.5 9.2 %all-to-all-start.1 = ((bf16[384,8,256]{0,2,1:T(8,128)(2,1)}), bf16[384,8,256]{0,2,1:T(8,128)(2,1)S(1)}, u32[]{:S(2)}, u32[]{:S(2)}) async-start(bf16[384,8,256]{0,2,1:T(8,128)(2,1)} %all-reduce.2.cloned.1.call-done), calls=%async_computation.1 | async-start | bytes 3145728 | tf_op jit(solution)/shard_map/all_to_all | solution.py:21
  105.7 0.1 reshape.21
  105.8 59.0 %all-to-all-done.1 = bf16[384,8,256]{0,2,1:T(8,128)(2,1)S(1)} async-done(((bf16[384,8,256]{0,2,1:T(8,128)(2,1)}), bf16[384,8,256]{0,2,1:T(8,128)(2,1)S(1)}, u32[]{:S(2)}, u32[]{:S(2)}) %all-to-all-start.1) | async-done | bytes 1572896 | tf_op jit(solution)/shard_map/all_to_all | solution.py:21
  164.8 0.7 copy.4
  165.5 20.7 %all-gather.2.cloned.1.call-done = bf16[3072,2048]{1,0:T(8,128)(2,1)} async-done(((bf16[384,2048]{1,0:T(8,128)(2,1)}), bf16[3072,2048]{1,0:T(8,128)(2,1)}) %all-gather.2.cloned.1.call-update) | async-done | bytes 12582928 | tf_op jit(solution)/shard_map/all_gather | solution.py:22
  186.2 10.6 %fusion = f32[2048,256]{1,0:T(8,128)} fusion(bf16[3072,256]{1,0:T(8,128)(2,1)S(1)} %bitcast.7, bf16[3072,2048]{1,0:T(8,128)(2,1)} %all-gather.2.cloned.1.call-done, f32[3072]{0:T(1024)S(1)} %bitcast.8), kind=kOutput, calls=%fused_computation.1 | convolution fusion | flops 3240099840 | bytes 16265216 | tf_op jit(solution)/shard_map/dot_general | solution.py:13
  (3 shorter events, 0.0 us)
Async XLA Ops:
  7.4 89.1 %all-reduce.2.cloned.1.call-start = ((), (), s32[]{:S(2)}) async-start(), calls=%async_computation.3 | async-start | bytes 3145728 | tf_op jit(solution)/shard_map/psum | solution.py:9
  10.5 0.7 copy-start
  10.6 175.6 %all-gather.2.cloned.1.call-start = ((), (), s32[]{:S(2)}) async-start(), calls=%async_computation.2 | async-start | bytes 14155776 | tf_op jit(solution)/shard_map/all_gather | solution.py:22
  96.5 68.3 %all-to-all-start.1 = ((bf16[384,8,256]{0,2,1:T(8,128)(2,1)}), bf16[384,8,256]{0,2,1:T(8,128)(2,1)S(1)}, u32[]{:S(2)}, u32[]{:S(2)}) async-start(bf16[384,8,256]{0,2,1:T(8,128)(2,1)} %all-reduce.2.cloned.1.call-done), calls=%async_computation.1 | async-start | bytes 3145728 | tf_op jit(solution)/shard_map/all_to_all | solution.py:21
Sparse Core Ops, SparseCore 0:
  10.7 85.7 all-reduce.1
Sparse Core Ops, SparseCore 1:
  13.1 173.0 all-gather.1
